TPU v7x, 512 devices: a whole 4x8x8 slice. The times are simulated.
512 devices in a mesh: rows: 16 (over x, y_hi, core), cols: 32 (over y_lo, z).
Axes of the slice: x: 4, y: 8 (y_hi: 2, y_lo: 4; y = y_hi * 4 + y_lo), z: 8, core: 2. Of those that a mesh axis runs over, the one named last changes fastest.
Arguments:
- field: bfloat16 [32, 64, 32768], P('cols', 'rows'), may hold values from -6 to 6
- depth_kernel: float32 [7, 7, 32], replicated, may hold values from -0.875 to 0.875
- point_weight: bfloat16 [32, 32], replicated, may hold values from -1 to 1
- point_bias: float32 [32], replicated, may hold values from -3 to 3
- vert_weight: bfloat16 [2, 288, 32], replicated, may hold values from -0.375 to 0.375
- vert_bias: float32 [2, 32], replicated, may hold values from -3 to 3
- exhaust: bfloat16 [262144, 32], P(('rows', 'cols')), may hold values from -6 to 6
- owner: int32 [262144, 1], P(('rows', 'cols')), may hold values from 0 to 31; in each aligned block of 512 rows (0 to 511, 512 to 1023, ...) at most 32 rows name the same one
- cells: int32 [262144], P(('rows', 'cols')), may hold values from 0 to 4095
Outputs:
- advanced: bfloat16 [32, 64, 32768], P(None, 'rows', 'cols')
Inputs may be any that keep to these rules, and one draw needn't show every extreme that they name: `owner`: among the 512 rows of one device, no tile is named by more than 32 rows, a bound that some block reaches.
All inputs are finite; a program needn't handle non-finite values.
Results may differ from a plain program's by a relative error of at most 0.0055.
Values may be sent and summed in bfloat16 or wider, within the bound.
A program may use at most 128 MiB of HBM per device.

v0:
```python
import jax
import jax.numpy as jnp
from jax import lax
from jax.sharding import PartitionSpec as P

C = 32
X = 1024
Z = 32
YB = 4
KH = 7
KV = 9
LAYERS = 2


def padded_2(block, sides, width):
    for axis, dim in sides:
        count = lax.axis_size(axis)
        forward = [(i, i + 1) for i in range(count - 1)]
        backward = [(target, source) for source, target in forward]
        low = lax.ppermute(
            lax.slice_in_dim(block, block.shape[dim] - width, None, axis=dim), axis, forward
        )
        high = lax.ppermute(lax.slice_in_dim(block, 0, width, axis=dim), axis, backward)
        block = jnp.concatenate([low, block, high], axis=dim)
    return block


def block_matrix(weight):
    return jnp.kron(jnp.eye(128 // C, dtype=jnp.bfloat16), weight)


def horizontal(band, depth_kernel, point_weight, point_bias):
    height = band.shape[1] - 6
    merged = band.shape[2] - 6 * C
    tiled = jnp.tile(depth_kernel, (1, 1, merged // C))
    total = jnp.zeros((band.shape[0], height, merged), jnp.float32)
    for i in range(KH):
        for j in range(KH):
            total = (
                total
                + band[:, i : i + height, j * C : j * C + merged].astype(jnp.float32) * tiled[i, j]
            )
    depth_b = total.astype(jnp.bfloat16).reshape(band.shape[0], height, merged // 128, 128)
    proj = jnp.einsum(
        "zywk,kd->zywd", depth_b, block_matrix(point_weight), preferred_element_type=jnp.float32
    )
    proj = proj.reshape(band.shape[0], height, merged)
    bias_row = jnp.tile(point_bias, merged // C)
    center = band[:, 3 : 3 + height, 3 * C : 3 * C + merged].astype(jnp.float32)
    return (center + jax.nn.gelu(proj + bias_row)).astype(jnp.bfloat16)


def vertical(level_field, vert_weight, vert_bias):
    levels = level_field.shape[0]
    height = level_field.shape[1]
    merged = level_field.shape[2]
    current = level_field.reshape(levels, height, merged // 128, 128)
    result = None
    for layer in range(LAYERS):
        padded = jnp.pad(current, ((4, 4), (0, 0), (0, 0), (0, 0)))
        conv = jnp.zeros(current.shape, jnp.float32)
        for k in range(KV):
            conv = conv + jnp.einsum(
                "zywk,kd->zywd",
                padded[k : k + levels],
                block_matrix(vert_weight[layer, k * C : (k + 1) * C]),
                preferred_element_type=jnp.float32,
            )
        bias_row = jnp.tile(vert_bias[layer], 128 // C)
        result = current.astype(jnp.float32) + jax.nn.gelu(conv + bias_row)
        if layer < LAYERS - 1:
            current = result.astype(jnp.bfloat16)
    return result.reshape(levels, height, merged)


def body(
    field, depth_kernel, point_weight, point_bias, vert_weight, vert_bias, exhaust, owner, cells
):
    columns = lax.axis_size("cols")
    tile_x = X // columns
    rimmed = padded_2(field, (("rows", 1),), 3)
    band = jnp.pad(rimmed, ((0, 0), (0, 0), (3 * C, 3 * C)))
    mixed = horizontal(band, depth_kernel, point_weight, point_bias)
    pre = vertical(
        lax.all_to_all(mixed, "cols", split_axis=2, concat_axis=0, tiled=True),
        vert_weight,
        vert_bias,
    )
    where_to = owner[:, 0]
    got_rows, got_owner, got_cells = (
        lax.all_gather(exhaust, "cols", axis=0, tiled=True),
        lax.all_gather(where_to, "cols", axis=0, tiled=True),
        lax.all_gather(cells, "cols", axis=0, tiled=True),
    )
    valid = got_owner == lax.axis_index("cols")
    tile_cells = Z * YB * tile_x
    target = jnp.where(valid, got_cells, tile_cells)
    source = (
        jnp.zeros((tile_cells, C), jnp.float32)
        .at[target]
        .add(got_rows.astype(jnp.float32), mode="drop")
    )
    source = source.reshape(Z, YB, tile_x * C)
    return (pre + source).astype(jnp.bfloat16)


def solution(mesh):
    placed = (
        P("cols", "rows", None),
        P(),
        P(),
        P(),
        P(),
        P(),
        P(("rows", "cols"), None),
        P(("rows", "cols"), None),
        P(("rows", "cols")),
    )
    return jax.shard_map(
        body, mesh=mesh, in_specs=placed, out_specs=P(None, "rows", "cols"), check_vma=False
    )
```

profile of v0, /device:TPU:6, one launch (start us, length us, event | category | flops | bytes accessed | tf_op | source)
XLA Modules:
  0.0 668.0 jit_solution(13744566044077631644)
XLA Ops:
  6.5 2.0 fusion.88
  8.6 1.9 collective-permute-start
  10.5 8.4 %collective-permute-start.1 = (bf16[1,3,32768]{2,1,0:T(4,128)(2,1)}, bf16[1,3,32768]{2,1,0:T(4,128)(2,1)S(1)}, u32[]{:S(2)}, u32[]{:S(2)}) collective-permute-start(bf16[1,3,32768]{2,1,0:T(4,128)(2,1)} %get-tuple-element.55), channel_id=1, source_target_pairs={{32,0},{64,32},{96,64},{128,96},{160,128},{192,160},{224,192},{256... | collective-permute-start | bytes 589832 | tf_op jit(solution)/shard_map/ppermute | solution.py:23
  19.0 10.9 %tile.14 = f32[7,7,1024,32]{3,2,1,0:T(8,128)} broadcast(f32[7,7,32]{2,1,0:T(8,128)} %param.10), dimensions={0,1,3} | broadcast | bytes 6428800 | tf_op jit(solution)/shard_map/tile | solution.py:35
  29.9 16.6 %tile.30 = f32[7,7,32768]{2,1,0:T(8,128)} reshape(f32[7,7,1024,32]{3,2,1,0:T(8,128)} %tile.14) | data formatting | bytes 12845056 | tf_op jit(solution)/shard_map/tile | solution.py:35
  46.5 11.1 %fusion.85 = (f32[1,1,32768]{2,1,0:T(1,128)S(1)}, f32[1,1,32768]{2,1,0:T(1,128)S(1)}, f32[1,1,32768]{2,1,0:T(1,128)S(1)}, f32[1,1,32768]{2,1,0:T(1,128)S(1)}, f3...) fusion(f32[7,7,32768]{2,1,0:T(8,128)} %tile.30), kind=kLoop, calls=%fused_computation.164 | loop fusion | bytes 4980736 | tf_op jit(solution)/shard_map/slice | solution.py:41
  57.6 11.4 %fusion.86 = (f32[1,1,32768]{2,1,0:T(1,128)}, f32[1,1,32768]{2,1,0:T(1,128)}, f32[1,1,32768]{2,1,0:T(1,128)}, f32[1,1,32768]{2,1,0:T(1,128)}, f32[1,1,32768]{2,1...) fusion(f32[7,7,32768]{2,1,0:T(8,128)} %tile.30), kind=kLoop, calls=%fused_computation.165 | loop fusion | bytes 4980736 | tf_op jit(solution)/shard_map/slice | solution.py:41
  69.1 7.6 %fusion.87 = (f32[1,1,32768]{2,1,0:T(1,128)}, f32[1,1,32768]{2,1,0:T(1,128)}, f32[1,1,32768]{2,1,0:T(1,128)}, f32[1,1,32768]{2,1,0:T(1,128)}, f32[1,1,32768]{2,1...) fusion(f32[7,7,32768]{2,1,0:T(8,128)} %tile.30), kind=kLoop, calls=%fused_computation.166 | loop fusion | bytes 2883584 | tf_op jit(solution)/shard_map/slice | solution.py:41
  76.8 0.4 copy-done.54
  77.2 0.7 reshape.359
  77.9 0.8 add.339
  78.8 1.0 slice_bitcast_fusion
  80.0 0.7 copy.305
  80.7 0.7 copy.306
  81.3 0.7 copy.307
  82.0 0.7 copy.310
  82.7 0.7 copy.311
  83.4 0.7 copy.312
  84.1 0.7 copy.313
  84.7 0.7 copy.314
  85.4 0.7 copy.315
  86.1 0.7 copy.316
  86.8 0.7 copy.317
  87.4 0.7 copy.318
  88.1 0.7 copy.319
  88.8 0.7 copy.320
  89.5 0.7 copy.321
  90.1 0.7 copy.322
  90.8 89.4 %all-gather = s32[16384,1]{0,1:T(1,128)} all-gather(s32[512,1]{0,1:T(1,128)} %param.16), channel_id=2, replica_groups=mesh['rows'=16,'cols'=32] {'cols'}, dimensions={0}, use_global_device_ids=true | all-gather | bytes 67584 | tf_op jit(solution)/shard_map/all_gather | solution.py:92
  180.5 3.2 broadcast_multiply_fusion
  183.7 0.8 slice_bitcast_fusion.18
  184.5 1.1 fusion.7
  185.9 10.3 %fusion.54 = bf16[1,4,256,128]{3,1,2,0:T(4,128)(2,1)S(1)} fusion(f32[32768]{0:T(1024)S(1)} %bitcast.195, bf16[1,10,32960]{2,1,0:T(8,128)(2,1)S(1)} %fusion.7, f32[32768]{0:T(1024)S(1)} %bitcast.196, f32[32768]{0:T(1024)S(1)} %bitcast.197, f32[32768]{0:T(1024)S(1)} %bitcast.198, bf16[1,3,32768]{2,1,0:T(4,128)(2,1)S(1)} %collective-permute-done.1, ...), kind=kLoop, calls=%fused_computation.92 | loop fusion | flops 21626880 | bytes 18350080
  196.6 1.4 fusion.22
  198.0 25.6 %copy.300 = bf16[1,4,32768]{1,0,2:T(2,128)(2,1)} copy(bf16[1,4,32768]{2,1,0:T(4,128)(2,1)S(1)} %fusion.22) | data formatting | bytes 524288 | tf_op jit(solution)/shard_map/convert_element_type | solution.py:50
  223.6 0.5 broadcast.203
  224.1 179.2 %reduce.2 = bf16[32768,4]{1,0:T(8,128)(2,1)} reduce(bf16[32768,1,4]{2,1,0:T(2,128)(2,1)} %bitcast.181, bf16[]{:T(256)} %broadcast.203), dimensions={1}, to_apply=%bitcast.168.reduce_sub_computation | reduce | bytes 524290
  403.4 16.9 %reshape.401 = bf16[32,2,2048]{2,1,0:T(2,128)(2,1)} reshape(bf16[32768,4]{1,0:T(8,128)(2,1)} %reduce.2) | data formatting | bytes 524288
  420.4 4.2 all-to-all-start
  427.5 78.6 %all-gather.1 = s32[32,1,512]{2,1,0:T(1,128)S(1)} all-gather(s32[1,1,512]{2,1,0:T(1,128)S(1)} %bitcast.244), channel_id=1, replica_groups=mesh['rows'=16,'cols'=32] {'cols'}, dimensions={0}, use_global_device_ids=true | all-gather | bytes 67584 | tf_op jit(solution)/shard_map/all_gather | solution.py:93
  506.2 24.2 %reshape.402 = bf16[32768,1,4]{2,1,0:T(2,128)(2,1)} reshape(bf16[32,2,2048]{2,1,0:T(2,128)(2,1)S(1)} %all-to-all-done) | data formatting | bytes 524288
  530.4 30.6 %copy.301 = bf16[1,4,32768]{2,1,0:T(4,128)(2,1)S(1)} copy(bf16[1,4,32768]{1,0,2:T(2,128)(2,1)} %bitcast.182) | data formatting | bytes 524288 | tf_op jit(solution)/shard_map/all_to_all | solution.py:85
  562.9 0.4 fusion.38
  565.1 0.4 fusion.46
  565.7 5.5 copy.323
  571.2 88.1 %scatter_custom_fusion = f32[4096,32]{1,0:T(8,128)S(1)} fusion(s32[16384]{0:T(1024)S(1)} %compare_select_fusion, f32[16384,32]{1,0:T(8,128)} %copy.323, f32[]{:T(128)} %constant.14.clone.1), kind=kCustom, calls=%fused_computation.27 | custom fusion | flops 524288 | bytes 524800 | tf_op jit(solution)/shard_map/scatter-add | solution.py:101
  659.3 0.9 reshape.344
  660.3 0.9 add_convert_fusion
  (169 shorter events, 7.4 us)
Async XLA Ops:
  6.5 559.2 %all-gather.4.cloned.1.call-start = ((), (), s32[]{:S(2)}) async-start(), calls=%async_computation.1 | async-start | bytes 1081344 | tf_op jit(solution)/shard_map/all_gather | solution.py:91
  8.6 175.9 %collective-permute-start = (bf16[1,3,32768]{2,1,0:T(4,128)(2,1)}, bf16[1,3,32768]{2,1,0:T(4,128)(2,1)S(1)}, u32[]{:S(2)}, u32[]{:S(2)}) collective-permute-start(bf16[1,3,32768]{2,1,0:T(4,128)(2,1)} %get-tuple-element.54), channel_id=1, source_target_pairs={{0,32},{32,64},{64,96},{96,128},{128,160},{160,192},{192,224},{224... | collective-permute-start | bytes 589832 | tf_op jit(solution)/shard_map/ppermute | solution.py:20
  10.5 174.0 %collective-permute-start.1 = (bf16[1,3,32768]{2,1,0:T(4,128)(2,1)}, bf16[1,3,32768]{2,1,0:T(4,128)(2,1)S(1)}, u32[]{:S(2)}, u32[]{:S(2)}) collective-permute-start(bf16[1,3,32768]{2,1,0:T(4,128)(2,1)} %get-tuple-element.55), channel_id=1, source_target_pairs={{32,0},{64,32},{96,64},{128,96},{160,128},{192,160},{224,192},{256... | collective-permute-start | bytes 589832 | tf_op jit(solution)/shard_map/ppermute | solution.py:23
  69.0 7.6 %copy-start.53 = (bf16[32,32]{1,0:T(8,128)(2,1)S(1)}, bf16[32,32]{1,0:T(8,128)(2,1)}, u32[]{:S(2)}) copy-start(bf16[32,32]{1,0:T(8,128)(2,1)} %param.11) | copy-start | bytes 6148
  69.0 8.9 %copy-start.56 = (f32[32]{0:T(128)S(1)}, f32[32]{0:T(128)}, u32[]{:S(2)}) copy-start(f32[32]{0:T(128)} %param.12) | copy-start | bytes 388
  77.9 106.6 %copy-start = (bf16[1,4,32768]{2,1,0:T(4,128)(2,1)S(1)}, bf16[1,4,32768]{2,1,0:T(4,128)(2,1)}, u32[]{:S(2)}) copy-start(bf16[1,4,32768]{2,1,0:T(4,128)(2,1)} %param.9) | copy-start | bytes 786436
  180.2 5.4 copy-start.5
  180.2 5.4 copy-start.6
  180.2 5.4 copy-start.7
  180.2 5.4 copy-start.8
  180.3 5.4 copy-start.9
  180.3 5.4 copy-start.10
  180.3 5.4 copy-start.11
  180.3 5.4 copy-start.12
  180.3 5.4 copy-start.13
  180.3 5.4 copy-start.14
  180.3 5.4 copy-start.15
  180.3 5.4 copy-start.16
  180.3 5.4 copy-start.17
  180.3 5.4 copy-start.18
  180.4 5.4 copy-start.19
  180.4 5.4 copy-start.20
  180.4 5.4 copy-start.21
  180.4 5.4 copy-start.22
  180.4 5.4 copy-start.23
  180.4 5.4 copy-start.24
  185.9 10.3 %copy-start.52 = (bf16[128,128,1]{1,0,2:T(8,128)(2,1)S(1)}, bf16[128,128,1]{1,0,2:T(8,128)(2,1)}, u32[]{:S(2)}) copy-start(bf16[128,128,1]{1,0,2:T(8,128)(2,1)} %reshape.359) | copy-start | bytes 98308
  403.3 21.3 %copy-start.51 = (s32[16384,1]{0,1:T(1,128)S(1)}, s32[16384,1]{0,1:T(1,128)}, u32[]{:S(2)}) copy-start(s32[16384,1]{0,1:T(1,128)} %all-gather) | copy-start | bytes 196612
  403.3 21.5 %copy-start.50 = (bf16[4,32,4,32]{3,2,1,0:T(4,128)(2,1)S(1)}, bf16[4,32,4,32]{3,2,1,0:T(4,128)(2,1)}, u32[]{:S(2)}) copy-start(bf16[4,32,4,32]{3,2,1,0:T(4,128)(2,1)} %get-tuple-element.75) | copy-start | bytes 98308
  403.3 21.7 %copy-start.49 = (bf16[4,32,4,32]{3,2,1,0:T(4,128)(2,1)S(1)}, bf16[4,32,4,32]{3,2,1,0:T(4,128)(2,1)}, u32[]{:S(2)}) copy-start(bf16[4,32,4,32]{3,2,1,0:T(4,128)(2,1)} %get-tuple-element.76) | copy-start | bytes 98308
  403.3 21.8 %copy-start.48 = (bf16[4,32,4,32]{3,2,1,0:T(4,128)(2,1)S(1)}, bf16[4,32,4,32]{3,2,1,0:T(4,128)(2,1)}, u32[]{:S(2)}) copy-start(bf16[4,32,4,32]{3,2,1,0:T(4,128)(2,1)} %get-tuple-element.77) | copy-start | bytes 98308
  403.3 21.9 %copy-start.47 = (bf16[4,32,4,32]{3,2,1,0:T(4,128)(2,1)S(1)}, bf16[4,32,4,32]{3,2,1,0:T(4,128)(2,1)}, u32[]{:S(2)}) copy-start(bf16[4,32,4,32]{3,2,1,0:T(4,128)(2,1)} %get-tuple-element.78) | copy-start | bytes 98308
  403.3 22.1 %copy-start.46 = (bf16[4,32,4,32]{3,2,1,0:T(4,128)(2,1)S(1)}, bf16[4,32,4,32]{3,2,1,0:T(4,128)(2,1)}, u32[]{:S(2)}) copy-start(bf16[4,32,4,32]{3,2,1,0:T(4,128)(2,1)} %get-tuple-element.79) | copy-start | bytes 98308
  403.3 22.2 %copy-start.45 = (bf16[4,32,4,32]{3,2,1,0:T(4,128)(2,1)S(1)}, bf16[4,32,4,32]{3,2,1,0:T(4,128)(2,1)}, u32[]{:S(2)}) copy-start(bf16[4,32,4,32]{3,2,1,0:T(4,128)(2,1)} %get-tuple-element.80) | copy-start | bytes 98308
  403.3 22.3 %copy-start.44 = (bf16[4,32,4,32]{3,2,1,0:T(4,128)(2,1)S(1)}, bf16[4,32,4,32]{3,2,1,0:T(4,128)(2,1)}, u32[]{:S(2)}) copy-start(bf16[4,32,4,32]{3,2,1,0:T(4,128)(2,1)} %get-tuple-element.81) | copy-start | bytes 98308
  403.4 22.5 %copy-start.43 = (bf16[4,32,4,32]{3,2,1,0:T(4,128)(2,1)S(1)}, bf16[4,32,4,32]{3,2,1,0:T(4,128)(2,1)}, u32[]{:S(2)}) copy-start(bf16[4,32,4,32]{3,2,1,0:T(4,128)(2,1)} %get-tuple-element.82) | copy-start | bytes 98308
  403.4 22.6 %copy-start.42 = (bf16[4,32,4,32]{3,2,1,0:T(4,128)(2,1)S(1)}, bf16[4,32,4,32]{3,2,1,0:T(4,128)(2,1)}, u32[]{:S(2)}) copy-start(bf16[4,32,4,32]{3,2,1,0:T(4,128)(2,1)} %get-tuple-element.83) | copy-start | bytes 98308
  420.3 5.9 copy-start.41
  420.3 6.0 copy-start.40
  420.3 6.1 copy-start.39
  420.3 6.3 copy-start.38
  420.3 6.4 copy-start.37
  420.3 6.5 copy-start.36
  420.3 6.7 copy-start.35
  420.3 6.8 %copy-start.34 = (bf16[4,32,4,32]{3,2,1,0:T(4,128)(2,1)S(1)}, bf16[4,32,4,32]{3,2,1,0:T(4,128)(2,1)}, u32[]{:S(2)}) copy-start(bf16[4,32,4,32]{3,2,1,0:T(4,128)(2,1)} %get-tuple-element.91) | copy-start | bytes 98308
  420.4 6.9 %copy-start.33 = (bf16[4,32,4,32]{3,2,1,0:T(4,128)(2,1)S(1)}, bf16[4,32,4,32]{3,2,1,0:T(4,128)(2,1)}, u32[]{:S(2)}) copy-start(bf16[4,32,4,32]{3,2,1,0:T(4,128)(2,1)} %get-tuple-element.74) | copy-start | bytes 98308
  420.4 7.2 %copy-start.55 = (s32[512]{0:T(512)S(1)}, s32[512]{0:T(512)}, u32[]{:S(2)}) copy-start(s32[512]{0:T(512)} %param.17) | copy-start | bytes 6148
  420.4 85.8 %all-to-all-start = ((bf16[32,2,2048]{2,1,0:T(2,128)(2,1)}), bf16[32,2,2048]{2,1,0:T(2,128)(2,1)S(1)}, u32[]{:S(2)}, u32[]{:S(2)}) async-start(bf16[32,2,2048]{2,1,0:T(2,128)(2,1)} %reshape.401), calls=%async_computation | async-start | bytes 524288 | tf_op jit(solution)/shard_map/all_to_all | solution.py:85
  (13 other events, 65.1 us)
Sparse Core Ops, SparseCore 0:
  19.1 157.3 all-gather.3
where the time goes:
time: 669 us; the launch traced here: 668 us
  other arithmetic  284 us (42%)
  local copies, waits for them, and re-layouts  182 us (27%)
  blocking collectives  168 us (25%)
  starting transfers between devices  14.6 us (2%)
  between operations  14.6 us (2%)
    unnamed x2, other arithmetic  189 us
    all_gather x1, blocking collectives, body(): lax.all_gather(where_to, 'cols', axis=0, tiled=True)  89.4 us
    scatter-add x1, other arithmetic, body(): source = jnp.zeros((tile_cells, C), jnp.float32).at[target].add(got_rows....  88.1 us
    all_gather x1, blocking collectives, body(): lax.all_gather(cells, 'cols', axis=0, tiled=True)  78.6 us
    unnamed x119, local copies, waits for them, and re-layouts  42.4 us
    all_to_all x1, local copies, waits for them, and re-layouts, body(): lax.all_to_all(mixed, 'cols', split_axis=2, concat_axis=0, tiled=True)  30.6 us
    slice x3, local copies, waits for them, and re-layouts, horizontal(): tiled[i, j]  30.1 us
    another operation x2, local copies, waits for them, and re-layouts, horizontal(): tiled = jnp.tile(depth_kernel, (1, 1, merged // C))  27.5 us
  transfers between devices with their start and end apart: 4, of which 0 were waited for; matrix products, arithmetic and copies ran while one was open for 56% of the time, Pallas kernels for 0%

commit v1 on v0

v1 whole, which is shorter than its diff:
```python
import jax
import jax.numpy as jnp
from jax import lax
from jax.experimental import pallas as pl
from jax.experimental.pallas import tpu as pltpu
from jax.sharding import PartitionSpec as P

C = 32
X = 1024
Z = 32
YB = 4
KH = 7
KV = 9
LAYERS = 2
E_DEV = 512
N_ROWS = 16
N_COLS = 32
LANES = 128
TILES = X * C // LANES
MSG = YB * TILES // N_COLS
MESH = pl.DeviceIdType.MESH
BF = jnp.bfloat16
F32 = jnp.float32
HIGH = lax.Precision.HIGHEST


def iota(shape, dim):
    return lax.broadcasted_iota(jnp.int32, shape, dim)


def dot(a, b):
    return jnp.dot(a, b, preferred_element_type=F32)


def select_matrix(rows, lanes):
    return iota((rows, lanes), 0) == iota((rows, lanes), 1) % rows


def lane_tile(x, lanes):
    return jnp.dot(
        x, select_matrix(C, lanes).astype(F32), preferred_element_type=F32, precision=HIGH
    )


def pack_exhaust(me, ex_ref, own_ref, cell_ref, xs):
    owner = own_ref[...]
    cell = cell_ref[...]
    onehot = iota((N_COLS, E_DEV), 0) == owner
    before = (iota((E_DEV, E_DEV), 0) < iota((E_DEV, E_DEV), 1)).astype(F32).astype(BF)
    earlier = dot(onehot.astype(F32).astype(BF), before)
    rank = jnp.sum(jnp.where(onehot, earlier, 0.0), axis=0, keepdims=True)
    rank_i = rank.astype(jnp.int32)
    level = cell >> 7
    y = (cell >> 5) & 3
    x = cell & 31
    low = ((x >> 2) << 2) + y
    zero = jnp.zeros((1, E_DEV), F32)
    values = jnp.concatenate(
        [level.astype(F32), low.astype(F32), (x & 3).astype(F32), rank, zero, zero, zero, zero],
        axis=0,
    )
    rank_col = jnp.transpose(values)[:, 3:4].astype(jnp.int32)
    lane = iota((E_DEV, LANES), 1)
    tiled = dot(ex_ref[...], select_matrix(C, LANES).astype(F32).astype(BF))
    placed = jnp.where(lane // C == rank_col // 8, tiled, 0.0).astype(BF)
    row = iota((N_COLS * 8, E_DEV), 0)
    to_row = (row == owner * 8 + rank_i % 8).astype(F32).astype(BF)
    data = dot(to_row, placed)
    spread = jnp.broadcast_to(values[None], (N_COLS, 8, E_DEV)).reshape(N_COLS * 8, E_DEV)
    meta_rows = jnp.where(row // 8 == owner, spread, 0.0).astype(BF)
    meta_lane = (lane == rank_col + (me % 4) * 32).astype(F32).astype(BF)
    meta = dot(meta_rows, meta_lane)
    xs[...] = jnp.concatenate(
        [data.reshape(N_COLS, 8, LANES), meta.reshape(N_COLS, 8, LANES)], axis=1
    ).astype(BF)


def add_exhaust(xr, codes, rows_b, source):
    got = xr[...].astype(F32)
    data = got[:, :8, :].reshape(N_COLS * 8, LANES).astype(BF)
    m = iota((LANES, 4 * LANES), 0)
    n = iota((LANES, 4 * LANES), 1)
    expand = ((m // C == n // LANES) & (m % C == n % C)).astype(F32).astype(BF)
    wide = dot(data, expand)
    by_slot = jnp.concatenate(
        [wide[:, g * LANES : (g + 1) * LANES].reshape(N_COLS, 1, 8, LANES) for g in range(4)],
        axis=1,
    ).reshape(N_COLS * 32, LANES)
    lane = iota((LANES, LANES), 1)
    for b in range(8):
        meta = got[4 * b, 8:, :]
        for k in range(1, 4):
            meta = meta + got[4 * b + k, 8:, :]
        codes[:, b * LANES : (b + 1) * LANES] = meta[0:1] * 32.0 + meta[1:2]
        place = jnp.transpose(meta)[:, 2:3].astype(jnp.int32)
        rows_b[b * LANES : (b + 1) * LANES, :] = jnp.where(
            lane // C == place, by_slot[b * LANES : (b + 1) * LANES, :], 0.0
        ).astype(BF)

    @pl.loop(0, 4)
    def _(block):
        base = pl.multiple_of(block * 256, 256)
        row = (iota((256, N_COLS * 32), 0) + base).astype(F32)
        hit = (row == codes[...]).astype(F32).astype(BF)
        source[pl.ds(base, 256), :] = dot(hit, rows_b[...])


def horizontal_weights(dk_ref, pw_ref, dk_pad, hw):
    for i in range(KH):
        dk_pad[i * 8 : i * 8 + KH, 0:C] = dk_ref[i]
    columns = jnp.transpose(dk_pad[...])[0:C, :]
    point = dot(pw_ref[...], select_matrix(C, 2 * LANES).astype(F32).astype(BF))
    block = iota((C, 2 * LANES), 1) // C
    for i in range(KH):
        taps = jnp.zeros((C, 2 * LANES), F32)
        for m in range(KH):
            j = KH - 1 - m
            taps = jnp.where(block == m, columns[:, i * 8 + j : i * 8 + j + 1], taps)
        taps = jnp.concatenate([taps * point, jnp.zeros((C, LANES), F32)], axis=1)
        for cell in range(4):
            start = i * LANES + cell * C
            hw[start : start + C, :] = pltpu.roll(taps, (cell + 1) * C, 1).astype(BF)


def vertical_weights(vw_ref, vw):
    row = iota((LANES, LANES), 0)
    lane = iota((LANES, LANES), 1)
    for layer in range(LAYERS):
        wide = dot(vw_ref[layer], select_matrix(C, LANES).astype(F32).astype(BF))
        for k in range(KV):
            part = wide[k * C : (k + 1) * C, :]
            whole = jnp.concatenate([part, part, part, part], axis=0)
            vw[layer, k * LANES : (k + 1) * LANES, :] = jnp.where(
                row // C == lane // C, whole, 0.0
            ).astype(BF)


def kernel(
    field_ref, dk_ref, pw_ref, pb_ref, vw_ref, vb_ref, ex_ref, own_ref, cell_ref, out_ref,
    stage, band, dk_pad, hw, vw, send, recv, mid, xs, xr, codes, rows_b, source,
    halo_send, halo_recv, mix_send, mix_recv, ex_send, ex_recv,
):
    r = lax.axis_index("rows")
    me = lax.axis_index("cols")
    barrier = pltpu.get_barrier_semaphore()

    @pl.loop(1, N_COLS)
    def _(s):
        pl.semaphore_signal(
            barrier, inc=1, device_id={"cols": lax.rem(me + s, N_COLS)}, device_id_type=MESH
        )

    for step in (1, N_ROWS - 1):
        pl.semaphore_signal(
            barrier, inc=1, device_id={"rows": lax.rem(r + step, N_ROWS)}, device_id_type=MESH
        )

    stage[...] = field_ref[...].astype(F32)
    for y in range(YB):
        band[3 + y] = stage[pl.ds(y, TILES, stride=YB), :].astype(BF)

    @pl.when(r == 0)
    def _():
        band[0:3] = jnp.zeros((3, TILES, LANES), BF)

    @pl.when(r == N_ROWS - 1)
    def _():
        band[7:10] = jnp.zeros((3, TILES, LANES), BF)

    pl.semaphore_wait(barrier, N_COLS + 1)

    to_next = pltpu.make_async_remote_copy(
        src_ref=band.at[4:7], dst_ref=band.at[0:3], send_sem=halo_send.at[0],
        recv_sem=halo_recv.at[0], device_id={"rows": lax.rem(r + 1, N_ROWS)},
        device_id_type=MESH,
    )
    to_last = pltpu.make_async_remote_copy(
        src_ref=band.at[3:6], dst_ref=band.at[7:10], send_sem=halo_send.at[1],
        recv_sem=halo_recv.at[1], device_id={"rows": lax.rem(r + N_ROWS - 1, N_ROWS)},
        device_id_type=MESH,
    )

    @pl.when(r < N_ROWS - 1)
    def _():
        to_next.start()

    @pl.when(r > 0)
    def _():
        to_last.start()

    pack_exhaust(me, ex_ref, own_ref, cell_ref, xs)

    def exhaust_copy(s):
        there = lax.rem(me + s, N_COLS)
        return pltpu.make_async_remote_copy(
            src_ref=xs.at[there], dst_ref=xr.at[me], send_sem=ex_send.at[there],
            recv_sem=ex_recv.at[me], device_id={"cols": there}, device_id_type=MESH,
        )

    def exhaust_arrival(s):
        there = lax.rem(me + s, N_COLS)
        return pltpu.make_async_remote_copy(
            src_ref=xs.at[there], dst_ref=xr.at[there], send_sem=ex_send.at[there],
            recv_sem=ex_recv.at[there], device_id={"cols": there}, device_id_type=MESH,
        )

    def mixed_copy(s):
        there = lax.rem(me + s, N_COLS)
        return pltpu.make_async_remote_copy(
            src_ref=send.at[there], dst_ref=recv.at[4 + me], send_sem=mix_send.at[there],
            recv_sem=mix_recv.at[me], device_id={"cols": there}, device_id_type=MESH,
        )

    def mixed_arrival(s):
        there = lax.rem(me + s, N_COLS)
        return pltpu.make_async_remote_copy(
            src_ref=send.at[there], dst_ref=recv.at[4 + there], send_sem=mix_send.at[there],
            recv_sem=mix_recv.at[there], device_id={"cols": there}, device_id_type=MESH,
        )

    @pl.loop(1, N_COLS)
    def _(s):
        exhaust_copy(s).start()

    xr[me] = xs[me]
    horizontal_weights(dk_ref, pw_ref, dk_pad, hw)
    vertical_weights(vw_ref, vw)
    bias_h = lane_tile(pb_ref[...], LANES)
    bias_v = lane_tile(vb_ref[...], LANES)
    edge = jnp.zeros((4, MSG, LANES), BF)
    for buffer in (recv, mid):
        buffer[0:4] = edge
        buffer[4 + Z : 8 + Z] = edge

    @pl.when(r > 0)
    def _():
        to_next.wait_recv()

    @pl.when(r < N_ROWS - 1)
    def _():
        to_last.wait_recv()

    row = iota((TILES, LANES), 0)
    for y in range(YB):
        rows = jnp.concatenate([band[y + i] for i in range(KH)], axis=1)
        parts = dot(rows, hw[...])
        right = pltpu.roll(parts[:, 0:LANES], TILES - 1, 0)
        left = pltpu.roll(parts[:, 2 * LANES : 3 * LANES], 1, 0)
        total = (
            parts[:, LANES : 2 * LANES]
            + jnp.where(row < TILES - 1, right, 0.0)
            + jnp.where(row > 0, left, 0.0)
        )
        stage[pl.ds(y, TILES, stride=YB), :] = band[3 + y].astype(F32) + jax.nn.gelu(
            total + bias_h
        )
    send[...] = stage[...].astype(BF).reshape(N_COLS, MSG, LANES)

    @pl.loop(1, N_COLS)
    def _(s):
        mixed_copy(s).start()

    recv[4 + me] = send[me]

    @pl.loop(1, N_COLS)
    def _(s):
        exhaust_arrival(s).wait_recv()

    add_exhaust(xr, codes, rows_b, source)

    @pl.loop(1, N_COLS)
    def _(s):
        mixed_arrival(s).wait_recv()

    def conv(buffer, layer, block):
        rows = jnp.concatenate(
            [buffer[pl.ds(block * 8 + k, 8)].reshape(8 * MSG, LANES) for k in range(KV)], axis=1
        )
        before = buffer[pl.ds(block * 8 + 4, 8)].reshape(8 * MSG, LANES).astype(F32)
        return before + jax.nn.gelu(dot(rows, vw[layer]) + bias_v[layer : layer + 1])

    @pl.loop(0, 4)
    def _(block):
        mid[pl.ds(block * 8 + 4, 8)] = conv(recv, 0, block).astype(BF).reshape(8, MSG, LANES)

    @pl.loop(0, 4)
    def _(block):
        base = pl.multiple_of(block * 256, 256)
        result = conv(mid, 1, block) + source[pl.ds(base, 256), :]
        out_ref[pl.ds(base, 256), :] = result.astype(BF)

    @pl.when(r < N_ROWS - 1)
    def _():
        to_next.wait_send()

    @pl.when(r > 0)
    def _():
        to_last.wait_send()

    @pl.loop(1, N_COLS)
    def _(s):
        exhaust_copy(s).wait_send()
        mixed_copy(s).wait_send()


def body(
    field, depth_kernel, point_weight, point_bias, vert_weight, vert_bias, exhaust, owner, cells
):
    rows = field.reshape(YB, TILES, LANES).transpose(1, 0, 2).reshape(TILES * YB, LANES)
    out = pl.pallas_call(
        kernel,
        out_shape=jax.ShapeDtypeStruct((Z * MSG, LANES), BF),
        in_specs=[pl.BlockSpec(memory_space=pltpu.VMEM)] * 9,
        out_specs=pl.BlockSpec(memory_space=pltpu.VMEM),
        scratch_shapes=[
            pltpu.VMEM((TILES * YB, LANES), F32),
            pltpu.VMEM((YB + 6, TILES, LANES), BF),
            pltpu.VMEM((LANES, LANES), F32),
            pltpu.VMEM((KH * LANES, 3 * LANES), BF),
            pltpu.VMEM((LAYERS, KV * LANES, LANES), BF),
            pltpu.VMEM((N_COLS, MSG, LANES), BF),
            pltpu.VMEM((Z + 8, MSG, LANES), BF),
            pltpu.VMEM((Z + 8, MSG, LANES), BF),
            pltpu.VMEM((N_COLS, 16, LANES), BF),
            pltpu.VMEM((N_COLS, 16, LANES), BF),
            pltpu.VMEM((1, N_COLS * 32), F32),
            pltpu.VMEM((N_COLS * 32, LANES), BF),
            pltpu.VMEM((Z * MSG, LANES), F32),
            pltpu.SemaphoreType.DMA((2,)),
            pltpu.SemaphoreType.DMA((2,)),
            pltpu.SemaphoreType.DMA((N_COLS,)),
            pltpu.SemaphoreType.DMA((N_COLS,)),
            pltpu.SemaphoreType.DMA((N_COLS,)),
            pltpu.SemaphoreType.DMA((N_COLS,)),
        ],
        compiler_params=pltpu.CompilerParams(
            collective_id=0, has_side_effects=True, vmem_limit_bytes=48 * 1024 * 1024
        ),
    )(
        rows, depth_kernel, point_weight, point_bias.reshape(1, C), vert_weight, vert_bias,
        exhaust, owner.reshape(1, E_DEV), cells.reshape(1, E_DEV),
    )
    return out.reshape(Z, MSG // YB, YB, LANES).transpose(0, 2, 1, 3).reshape(Z, YB, X * C // N_COLS)


def solution(mesh):
    placed = (
        P("cols", "rows", None),
        P(),
        P(),
        P(),
        P(),
        P(),
        P(("rows", "cols"), None),
        P(("rows", "cols"), None),
        P(("rows", "cols")),
    )
    return jax.shard_map(
        body, mesh=mesh, in_specs=placed, out_specs=P(None, "rows", "cols"), check_vma=False
    )
```

time: 669 us -> 42.3 us (0.06)
  the two profiles are of different devices: /device:TPU:6 before, /device:TPU:59 now
where the time goes in v1:
time: 42.3 us; the launch traced here: 42.1 us
  Pallas kernels  39.3 us (93%)
  local copies, waits for them, and re-layouts  2.65 us (6%)
    pallas_call x1, Pallas kernels, body(): pl.pallas_call(kernel, out_shape=jax.ShapeDtypeStruct((Z * MSG, LANES), B...  39.3 us
    unnamed x17, local copies, waits for them, and re-layouts  2.65 us

profile of v1, /device:TPU:59, one launch (start us, length us, event | category | flops | bytes accessed | tf_op | source)
XLA Modules:
  0.0 42.1 jit_solution(11141332662401272791)
XLA Ops:
  0.0 0.0 copy-start
  0.0 0.9 %copy.12.ex_ref = bf16[512,32]{1,0:T(8,128)(2,1)S(1)} copy(bf16[512,32]{0,1:T(8,128)(2,1)} %param.15) | data formatting | bytes 65536 | tf_op args[6]
  0.9 0.0 copy-start.1
  0.9 0.0 copy-start.2
  0.9 0.0 copy-start.3
  1.0 0.0 copy-start.4
  1.0 0.0 copy-start.5
  1.0 0.0 copy-start.6
  1.0 1.0 %copy.11.vw_ref = bf16[2,288,32]{2,1,0:T(8,128)(2,1)S(1)} copy(bf16[2,288,32]{1,2,0:T(8,128)(2,1)} %param.13) | data formatting | bytes 73728 | tf_op args[4]
  2.0 0.0 copy-done
  2.0 0.0 copy-done.1
  2.0 0.0 copy-done.2
  2.0 0.0 copy-done.3
  2.0 0.0 copy-done.4
  2.0 0.0 copy-done.5
  2.0 0.0 copy-done.6
  2.1 39.3 %shard_map.91 = bf16[1024,128]{1,0:T(8,128)(2,1)S(1)} custom-call(bf16[1024,128]{1,0:T(8,128)(2,1)S(1)} %bitcast.14, f32[7,7,32]{2,1,0:T(8,128)S(1)} %copy-done.1, bf16[32,32]{1,0:T(8,128)(2,1)S(1)} %copy-done.2, f32[1,32]{1,0:T(1,128)S(1)} %bitcast.17, bf16[2,288,32]{2,1,0:T(8,128)(2,1)S(1)} %copy.11.vw_ref, f32[2,32]{1,0:T(2,128)S(1)} %copy-done.5, ...), custom_call_target="tpu_custom_call" | custom-call | tf_op jit(solution)/shard_map/pallas_call | solution.py:310
  41.4 0.7 %copy.15 = bf16[32,4,1024]{2,1,0:T(4,128)(2,1)} copy(bf16[32,4,1024]{2,1,0:T(4,128)(2,1)S(1)} %bitcast.13) | data formatting | bytes 524288
Async XLA Ops:
  0.0 2.0 %copy-start = (bf16[1,4,32768]{2,1,0:T(4,128)(2,1)S(1)}, bf16[1,4,32768]{2,1,0:T(4,128)(2,1)}, u32[]{:S(2)}) copy-start(bf16[1,4,32768]{2,1,0:T(4,128)(2,1)} %param.9) | copy-start | bytes 786436
  0.9 1.1 %copy-start.1 = (f32[7,7,32]{2,1,0:T(8,128)S(1)}, f32[7,7,32]{2,1,0:T(8,128)}, u32[]{:S(2)}) copy-start(f32[7,7,32]{2,1,0:T(8,128)} %dk_ref.1) | copy-start | bytes 18820
  0.9 1.1 %copy-start.2 = (bf16[32,32]{1,0:T(8,128)(2,1)S(1)}, bf16[32,32]{1,0:T(8,128)(2,1)}, u32[]{:S(2)}) copy-start(bf16[32,32]{1,0:T(8,128)(2,1)} %pw_ref.1) | copy-start | bytes 6148
  0.9 1.1 %copy-start.3 = (s32[512,1]{0,1:T(1,128)S(1)}, s32[512,1]{0,1:T(1,128)}, u32[]{:S(2)}) copy-start(s32[512,1]{0,1:T(1,128)} %param.16) | copy-start | bytes 6148
  1.0 1.1 %copy-start.4 = (s32[512]{0:T(512)S(1)}, s32[512]{0:T(512)}, u32[]{:S(2)}) copy-start(s32[512]{0:T(512)} %param.17) | copy-start | bytes 6148
  1.0 1.1 %copy-start.5 = (f32[2,32]{1,0:T(2,128)S(1)}, f32[2,32]{1,0:T(2,128)}, u32[]{:S(2)}) copy-start(f32[2,32]{1,0:T(2,128)} %vb_ref.1) | copy-start | bytes 772
  1.0 1.1 %copy-start.6 = (f32[32]{0:T(128)S(1)}, f32[32]{0:T(128)}, u32[]{:S(2)}) copy-start(f32[32]{0:T(128)} %param.12) | copy-start | bytes 388

commit v2 on v1

--- a/solution.py
+++ b/solution.py
@@ -17,7 +17,9 @@
 N_COLS = 32
 LANES = 128
 TILES = X * C // LANES
-MSG = YB * TILES // N_COLS
+TILE = TILES // N_COLS
+MSG = YB * TILE
+GROUPS = (1, 2, 3, 4)
 MESH = pl.DeviceIdType.MESH
 BF = jnp.bfloat16
 F32 = jnp.float32
@@ -42,7 +44,7 @@
     )
 
 
-def pack_exhaust(me, ex_ref, own_ref, cell_ref, xs):
+def pack_exhaust(me, odd, ex_ref, own_ref, cell_ref, xs):
     owner = own_ref[...]
     cell = cell_ref[...]
     onehot = iota((N_COLS, E_DEV), 0) == owner
@@ -53,7 +55,7 @@
     level = cell >> 7
     y = (cell >> 5) & 3
     x = cell & 31
-    low = ((x >> 2) << 2) + y
+    low = (y * odd + (3 - y) * (1 - odd)) * TILE + (x >> 2)
     zero = jnp.zeros((1, E_DEV), F32)
     values = jnp.concatenate(
         [level.astype(F32), low.astype(F32), (x & 3).astype(F32), rank, zero, zero, zero, zero],
@@ -61,7 +63,8 @@
     )
     rank_col = jnp.transpose(values)[:, 3:4].astype(jnp.int32)
     lane = iota((E_DEV, LANES), 1)
-    tiled = dot(ex_ref[...], select_matrix(C, LANES).astype(F32).astype(BF))
+    columns = ex_ref[...].astype(F32)
+    tiled = jnp.transpose(jnp.concatenate([columns] * 4, axis=0))
     placed = jnp.where(lane // C == rank_col // 8, tiled, 0.0).astype(BF)
     row = iota((N_COLS * 8, E_DEV), 0)
     to_row = (row == owner * 8 + rank_i % 8).astype(F32).astype(BF)
@@ -122,11 +125,14 @@
             hw[start : start + C, :] = pltpu.roll(taps, (cell + 1) * C, 1).astype(BF)
 
 
-def vertical_weights(vw_ref, vw):
+def vertical_weights(vw_ref, vw_pad, vw):
     row = iota((LANES, LANES), 0)
     lane = iota((LANES, LANES), 1)
     for layer in range(LAYERS):
-        wide = dot(vw_ref[layer], select_matrix(C, LANES).astype(F32).astype(BF))
+        taps = vw_ref[layer].astype(F32)
+        for copy in range(4):
+            vw_pad[copy * C : (copy + 1) * C, 0 : KV * C] = taps
+        wide = jnp.transpose(vw_pad[...])
         for k in range(KV):
             part = wide[k * C : (k + 1) * C, :]
             whole = jnp.concatenate([part, part, part, part], axis=0)
@@ -137,12 +143,19 @@
 
 def kernel(
     field_ref, dk_ref, pw_ref, pb_ref, vw_ref, vb_ref, ex_ref, own_ref, cell_ref, out_ref,
-    stage, band, dk_pad, hw, vw, send, recv, mid, xs, xr, codes, rows_b, source,
-    halo_send, halo_recv, mix_send, mix_recv, ex_send, ex_recv,
+    stage, band, dk_pad, hw, vw_pad, vw, send, recv, mid, xs, xr, codes, rows_b, source,
+    near_send, near_recv, far_send, far_recv, mix_send, mix_recv, ex_send, ex_recv,
 ):
     r = lax.axis_index("rows")
     me = lax.axis_index("cols")
+    odd = lax.rem(r, 2)
+    near = r + 1 - 2 * odd
+    far = lax.rem(r + N_ROWS - 1 + 2 * odd, N_ROWS)
+    has_far = jnp.logical_and(r > 0, r < N_ROWS - 1)
     barrier = pltpu.get_barrier_semaphore()
+
+    for row in (near, far):
+        pl.semaphore_signal(barrier, inc=1, device_id={"rows": row}, device_id_type=MESH)
 
     @pl.loop(1, N_COLS)
     def _(s):
@@ -150,11 +163,6 @@
             barrier, inc=1, device_id={"cols": lax.rem(me + s, N_COLS)}, device_id_type=MESH
         )
 
-    for step in (1, N_ROWS - 1):
-        pl.semaphore_signal(
-            barrier, inc=1, device_id={"rows": lax.rem(r + step, N_ROWS)}, device_id_type=MESH
-        )
-
     stage[...] = field_ref[...].astype(F32)
     for y in range(YB):
         band[3 + y] = stage[pl.ds(y, TILES, stride=YB), :].astype(BF)
@@ -169,62 +177,59 @@
 
     pl.semaphore_wait(barrier, N_COLS + 1)
 
-    to_next = pltpu.make_async_remote_copy(
-        src_ref=band.at[4:7], dst_ref=band.at[0:3], send_sem=halo_send.at[0],
-        recv_sem=halo_recv.at[0], device_id={"rows": lax.rem(r + 1, N_ROWS)},
-        device_id_type=MESH,
-    )
-    to_last = pltpu.make_async_remote_copy(
-        src_ref=band.at[3:6], dst_ref=band.at[7:10], send_sem=halo_send.at[1],
-        recv_sem=halo_recv.at[1], device_id={"rows": lax.rem(r + N_ROWS - 1, N_ROWS)},
-        device_id_type=MESH,
-    )
-
-    @pl.when(r < N_ROWS - 1)
+    near_copy = pltpu.make_async_remote_copy(
+        src_ref=band.at[pl.ds(4 - odd, 3)], dst_ref=band.at[pl.ds(7 * odd, 3)],
+        send_sem=near_send, recv_sem=near_recv, device_id={"rows": near}, device_id_type=MESH,
+    )
+    near_arrival = pltpu.make_async_remote_copy(
+        src_ref=band.at[pl.ds(4 - odd, 3)], dst_ref=band.at[pl.ds(7 * (1 - odd), 3)],
+        send_sem=near_send, recv_sem=near_recv, device_id={"rows": near}, device_id_type=MESH,
+    )
+
+    def far_copy(j):
+        return pltpu.make_async_remote_copy(
+            src_ref=band.at[odd * (7 - j) + (1 - odd) * (2 + j)],
+            dst_ref=band.at[odd * (3 - j) + (1 - odd) * (6 + j)],
+            send_sem=far_send.at[j - 1], recv_sem=far_recv.at[j - 1],
+            device_id={"rows": far}, device_id_type=MESH,
+        )
+
+    def far_arrival(j):
+        return pltpu.make_async_remote_copy(
+            src_ref=band.at[odd * (7 - j) + (1 - odd) * (2 + j)],
+            dst_ref=band.at[odd * (6 + j) + (1 - odd) * (3 - j)],
+            send_sem=far_send.at[j - 1], recv_sem=far_recv.at[j - 1],
+            device_id={"rows": far}, device_id_type=MESH,
+        )
+
+    @pl.when(has_far)
     def _():
-        to_next.start()
-
-    @pl.when(r > 0)
-    def _():
-        to_last.start()
-
-    pack_exhaust(me, ex_ref, own_ref, cell_ref, xs)
-
-    def exhaust_copy(s):
-        there = lax.rem(me + s, N_COLS)
-        return pltpu.make_async_remote_copy(
-            src_ref=xs.at[there], dst_ref=xr.at[me], send_sem=ex_send.at[there],
-            recv_sem=ex_recv.at[me], device_id={"cols": there}, device_id_type=MESH,
-        )
-
-    def exhaust_arrival(s):
-        there = lax.rem(me + s, N_COLS)
-        return pltpu.make_async_remote_copy(
-            src_ref=xs.at[there], dst_ref=xr.at[there], send_sem=ex_send.at[there],
-            recv_sem=ex_recv.at[there], device_id={"cols": there}, device_id_type=MESH,
-        )
-
-    def mixed_copy(s):
-        there = lax.rem(me + s, N_COLS)
-        return pltpu.make_async_remote_copy(
-            src_ref=send.at[there], dst_ref=recv.at[4 + me], send_sem=mix_send.at[there],
-            recv_sem=mix_recv.at[me], device_id={"cols": there}, device_id_type=MESH,
-        )
-
-    def mixed_arrival(s):
-        there = lax.rem(me + s, N_COLS)
-        return pltpu.make_async_remote_copy(
-            src_ref=send.at[there], dst_ref=recv.at[4 + there], send_sem=mix_send.at[there],
-            recv_sem=mix_recv.at[there], device_id={"cols": there}, device_id_type=MESH,
-        )
+        for j in range(1, 4):
+            far_copy(j).start()
+
+    near_copy.start()
+    pack_exhaust(me, odd, ex_ref, own_ref, cell_ref, xs)
 
     @pl.loop(1, N_COLS)
     def _(s):
-        exhaust_copy(s).start()
+        there = lax.rem(me + s, N_COLS)
+        pltpu.make_async_remote_copy(
+            src_ref=xs.at[there], dst_ref=xr.at[me], send_sem=ex_send, recv_sem=ex_recv,
+            device_id={"cols": there}, device_id_type=MESH,
+        ).start()
+
+    all_exhaust = pltpu.make_async_remote_copy(
+        src_ref=xs.at[0 : N_COLS - 1], dst_ref=xr.at[0 : N_COLS - 1], send_sem=ex_send,
+        recv_sem=ex_recv, device_id={"cols": lax.rem(me + 1, N_COLS)}, device_id_type=MESH,
+    )
+    all_mixed = pltpu.make_async_remote_copy(
+        src_ref=send.at[0 : N_COLS - 1], dst_ref=recv.at[4 : N_COLS + 3], send_sem=mix_send,
+        recv_sem=mix_recv, device_id={"cols": lax.rem(me + 1, N_COLS)}, device_id_type=MESH,
+    )
 
     xr[me] = xs[me]
     horizontal_weights(dk_ref, pw_ref, dk_pad, hw)
-    vertical_weights(vw_ref, vw)
+    vertical_weights(vw_ref, vw_pad, vw)
     bias_h = lane_tile(pb_ref[...], LANES)
     bias_v = lane_tile(vb_ref[...], LANES)
     edge = jnp.zeros((4, MSG, LANES), BF)
@@ -232,16 +237,10 @@
         buffer[0:4] = edge
         buffer[4 + Z : 8 + Z] = edge
 
-    @pl.when(r > 0)
-    def _():
-        to_next.wait_recv()
-
-    @pl.when(r < N_ROWS - 1)
-    def _():
-        to_last.wait_recv()
-
     row = iota((TILES, LANES), 0)
-    for y in range(YB):
+
+    def horizontal(slot):
+        y = odd * slot + (1 - odd) * (3 - slot)
         rows = jnp.concatenate([band[y + i] for i in range(KH)], axis=1)
         parts = dot(rows, hw[...])
         right = pltpu.roll(parts[:, 0:LANES], TILES - 1, 0)
@@ -251,26 +250,36 @@
             + jnp.where(row < TILES - 1, right, 0.0)
             + jnp.where(row > 0, left, 0.0)
         )
-        stage[pl.ds(y, TILES, stride=YB), :] = band[3 + y].astype(F32) + jax.nn.gelu(
-            total + bias_h
-        )
-    send[...] = stage[...].astype(BF).reshape(N_COLS, MSG, LANES)
-
-    @pl.loop(1, N_COLS)
-    def _(s):
-        mixed_copy(s).start()
+        mixed = band[3 + y].astype(F32) + jax.nn.gelu(total + bias_h)
+        send[:, slot * TILE : (slot + 1) * TILE, :] = mixed.astype(BF).reshape(N_COLS, TILE, LANES)
+
+    near_arrival.wait_recv()
+    first = 0
+    for slot in range(YB):
+        if slot > 0:
+
+            @pl.when(has_far)
+            def _():
+                far_arrival(slot).wait_recv()
+
+        horizontal(slot)
+        if slot + 1 in GROUPS:
+            part = slice(first * TILE, (slot + 1) * TILE)
+            first = slot + 1
+
+            @pl.loop(1, N_COLS)
+            def _(s):
+                there = lax.rem(me + s, N_COLS)
+                pltpu.make_async_remote_copy(
+                    src_ref=send.at[there, part], dst_ref=recv.at[4 + me, part],
+                    send_sem=mix_send, recv_sem=mix_recv, device_id={"cols": there},
+                    device_id_type=MESH,
+                ).start()
 
     recv[4 + me] = send[me]
-
-    @pl.loop(1, N_COLS)
-    def _(s):
-        exhaust_arrival(s).wait_recv()
-
+    all_exhaust.wait_recv()
     add_exhaust(xr, codes, rows_b, source)
-
-    @pl.loop(1, N_COLS)
-    def _(s):
-        mixed_arrival(s).wait_recv()
+    all_mixed.wait_recv()
 
     def conv(buffer, layer, block):
         rows = jnp.concatenate(
@@ -287,20 +296,24 @@
     def _(block):
         base = pl.multiple_of(block * 256, 256)
         result = conv(mid, 1, block) + source[pl.ds(base, 256), :]
-        out_ref[pl.ds(base, 256), :] = result.astype(BF)
-
-    @pl.when(r < N_ROWS - 1)
+        for level in range(8):
+            for slot in range(YB):
+                y = odd * slot + (1 - odd) * (3 - slot)
+                start = level * MSG + slot * TILE
+                stage[pl.ds(base + level * MSG + y, TILE, stride=YB), :] = result[
+                    start : start + TILE
+                ]
+        out_ref[pl.ds(base, 256), :] = stage[pl.ds(base, 256), :].astype(BF)
+
+    near_copy.wait_send()
+
+    @pl.when(has_far)
     def _():
-        to_next.wait_send()
-
-    @pl.when(r > 0)
-    def _():
-        to_last.wait_send()
-
-    @pl.loop(1, N_COLS)
-    def _(s):
-        exhaust_copy(s).wait_send()
-        mixed_copy(s).wait_send()
+        for j in range(1, 4):
+            far_copy(j).wait_send()
+
+    all_exhaust.wait_send()
+    all_mixed.wait_send()
 
 
 def body(
@@ -317,6 +330,7 @@
             pltpu.VMEM((YB + 6, TILES, LANES), BF),
             pltpu.VMEM((LANES, LANES), F32),
             pltpu.VMEM((KH * LANES, 3 * LANES), BF),
+            pltpu.VMEM((LANES, 3 * LANES), F32),
             pltpu.VMEM((LAYERS, KV * LANES, LANES), BF),
             pltpu.VMEM((N_COLS, MSG, LANES), BF),
             pltpu.VMEM((Z + 8, MSG, LANES), BF),
@@ -326,19 +340,21 @@
             pltpu.VMEM((1, N_COLS * 32), F32),
             pltpu.VMEM((N_COLS * 32, LANES), BF),
             pltpu.VMEM((Z * MSG, LANES), F32),
-            pltpu.SemaphoreType.DMA((2,)),
-            pltpu.SemaphoreType.DMA((2,)),
-            pltpu.SemaphoreType.DMA((N_COLS,)),
-            pltpu.SemaphoreType.DMA((N_COLS,)),
-            pltpu.SemaphoreType.DMA((N_COLS,)),
-            pltpu.SemaphoreType.DMA((N_COLS,)),
+            pltpu.SemaphoreType.DMA,
+            pltpu.SemaphoreType.DMA,
+            pltpu.SemaphoreType.DMA((3,)),
+            pltpu.SemaphoreType.DMA((3,)),
+            pltpu.SemaphoreType.DMA,
+            pltpu.SemaphoreType.DMA,
+            pltpu.SemaphoreType.DMA,
+            pltpu.SemaphoreType.DMA,
         ],
         compiler_params=pltpu.CompilerParams(
             collective_id=0, has_side_effects=True, vmem_limit_bytes=48 * 1024 * 1024
         ),
     )(
-        rows, depth_kernel, point_weight, point_bias.reshape(1, C), vert_weight, vert_bias,
-        exhaust, owner.reshape(1, E_DEV), cells.reshape(1, E_DEV),
+        rows, depth_kernel, point_weight, point_bias.reshape(1, C),
+        vert_weight.transpose(0, 2, 1), vert_bias, exhaust.T, owner.reshape(1, E_DEV), cells.reshape(1, E_DEV),
     )
     return out.reshape(Z, MSG // YB, YB, LANES).transpose(0, 2, 1, 3).reshape(Z, YB, X * C // N_COLS)
 

time: 42.3 us -> 43.8 us (1.035)
  the two profiles are of different devices: /device:TPU:59 before, /device:TPU:1 now
where the time goes in v2:
time: 43.8 us; the launch traced here: 43.4 us
  Pallas kernels  37.4 us (85%)
  local copies, waits for them, and re-layouts  6 us (14%)
    pallas_call x1, Pallas kernels, body(): pl.pallas_call(kernel, out_shape=jax.ShapeDtypeStruct((Z * MSG, LANES), B...  37.4 us
    unnamed x19, local copies, waits for them, and re-layouts  6 us

profile of v2, /device:TPU:1, one launch (start us, length us, event | category | flops | bytes accessed | tf_op | source)
XLA Modules:
  0.0 43.4 jit_solution(17305288942394748605)
XLA Ops:
  0.0 0.0 copy-start.4
  0.0 0.0 copy-start.5
  0.0 0.0 copy-start.7
  0.0 0.7 %copy-done.4 = bf16[32,32]{1,0:T(8,128)(2,1)S(1)} copy-done((bf16[32,32]{1,0:T(8,128)(2,1)S(1)}, bf16[32,32]{1,0:T(8,128)(2,1)}, u32[]{:S(2)}) %copy-start.4) | copy-done | bytes 2072
  0.7 0.0 copy-done.5
  0.7 0.0 copy-done.7
  0.7 0.0 copy-start
  0.7 0.9 %copy-done = bf16[1,4,32768]{2,1,0:T(4,128)(2,1)S(1)} copy-done((bf16[1,4,32768]{2,1,0:T(4,128)(2,1)S(1)}, bf16[1,4,32768]{2,1,0:T(4,128)(2,1)}, u32[]{:S(2)}) %copy-start) | copy-done | bytes 262168
  1.7 0.0 copy-start.1
  1.7 0.8 %copy-done.1 = bf16[2,288,32]{1,2,0:T(8,128)(2,1)S(1)} copy-done((bf16[2,288,32]{1,2,0:T(8,128)(2,1)S(1)}, bf16[2,288,32]{1,2,0:T(8,128)(2,1)}, u32[]{:S(2)}) %copy-start.1) | copy-done | bytes 36888
  2.5 0.0 copy-start.2
  2.5 0.8 %copy-done.2 = bf16[512,32]{0,1:T(8,128)(2,1)S(1)} copy-done((bf16[512,32]{0,1:T(8,128)(2,1)S(1)}, bf16[512,32]{0,1:T(8,128)(2,1)}, u32[]{:S(2)}) %copy-start.2) | copy-done | bytes 32792
  3.2 0.0 copy-start.3
  3.2 0.7 %copy-done.3 = f32[7,7,32]{2,1,0:T(8,128)S(1)} copy-done((f32[7,7,32]{2,1,0:T(8,128)S(1)}, f32[7,7,32]{2,1,0:T(8,128)}, u32[]{:S(2)}) %copy-start.3) | copy-done | bytes 6296
  4.0 0.0 copy-start.6
  4.0 0.7 %copy-done.6 = s32[512]{0:T(512)S(1)} copy-done((s32[512]{0:T(512)S(1)}, s32[512]{0:T(512)}, u32[]{:S(2)}) %copy-start.6) | copy-done | bytes 2072
  4.7 0.0 copy-start.8
  4.7 0.7 %copy-done.8 = f32[32]{0:T(128)S(1)} copy-done((f32[32]{0:T(128)S(1)}, f32[32]{0:T(128)}, u32[]{:S(2)}) %copy-start.8) | copy-done | bytes 152
  5.3 37.4 %shard_map.91 = bf16[1024,128]{1,0:T(8,128)(2,1)S(1)} custom-call(bf16[1024,128]{1,0:T(8,128)(2,1)S(1)} %bitcast.16, f32[7,7,32]{2,1,0:T(8,128)S(1)} %copy-done.3, bf16[32,32]{1,0:T(8,128)(2,1)S(1)} %copy-done.4, f32[1,32]{1,0:T(1,128)S(1)} %bitcast.21, bf16[2,32,288]{2,1,0:T(8,128)(2,1)S(1)} %bitcast.17, f32[2,32]{1,0:T(2,128)S(1)} %copy-done.7, ...), custom_call_target="tpu_custom_call" | custom-call | tf_op jit(solution)/shard_map/pallas_call | solution.py:323
  42.7 0.7 %copy.13 = bf16[32,4,1024]{2,1,0:T(4,128)(2,1)} copy(bf16[32,4,1024]{2,1,0:T(4,128)(2,1)S(1)} %bitcast.15) | data formatting | bytes 524288
Async XLA Ops:
  0.0 0.7 %copy-start.4 = (bf16[32,32]{1,0:T(8,128)(2,1)S(1)}, bf16[32,32]{1,0:T(8,128)(2,1)}, u32[]{:S(2)}) copy-start(bf16[32,32]{1,0:T(8,128)(2,1)} %pw_ref.1) | copy-start | bytes 6148
  0.0 0.7 %copy-start.5 = (s32[512,1]{0,1:T(1,128)S(1)}, s32[512,1]{0,1:T(1,128)}, u32[]{:S(2)}) copy-start(s32[512,1]{0,1:T(1,128)} %param.16) | copy-start | bytes 6148
  0.0 0.7 %copy-start.7 = (f32[2,32]{1,0:T(2,128)S(1)}, f32[2,32]{1,0:T(2,128)}, u32[]{:S(2)}) copy-start(f32[2,32]{1,0:T(2,128)} %vb_ref.1) | copy-start | bytes 772
  0.7 0.9 %copy-start = (bf16[1,4,32768]{2,1,0:T(4,128)(2,1)S(1)}, bf16[1,4,32768]{2,1,0:T(4,128)(2,1)}, u32[]{:S(2)}) copy-start(bf16[1,4,32768]{2,1,0:T(4,128)(2,1)} %param.9) | copy-start | bytes 786436
  1.7 0.8 %copy-start.1 = (bf16[2,288,32]{1,2,0:T(8,128)(2,1)S(1)}, bf16[2,288,32]{1,2,0:T(8,128)(2,1)}, u32[]{:S(2)}) copy-start(bf16[2,288,32]{1,2,0:T(8,128)(2,1)} %param.13) | copy-start | bytes 110596
  2.5 0.8 %copy-start.2 = (bf16[512,32]{0,1:T(8,128)(2,1)S(1)}, bf16[512,32]{0,1:T(8,128)(2,1)}, u32[]{:S(2)}) copy-start(bf16[512,32]{0,1:T(8,128)(2,1)} %param.15) | copy-start | bytes 98308
  3.2 0.7 %copy-start.3 = (f32[7,7,32]{2,1,0:T(8,128)S(1)}, f32[7,7,32]{2,1,0:T(8,128)}, u32[]{:S(2)}) copy-start(f32[7,7,32]{2,1,0:T(8,128)} %dk_ref.1) | copy-start | bytes 18820
  4.0 0.7 %copy-start.6 = (s32[512]{0:T(512)S(1)}, s32[512]{0:T(512)}, u32[]{:S(2)}) copy-start(s32[512]{0:T(512)} %param.17) | copy-start | bytes 6148
  4.7 0.7 %copy-start.8 = (f32[32]{0:T(128)S(1)}, f32[32]{0:T(128)}, u32[]{:S(2)}) copy-start(f32[32]{0:T(128)} %param.12) | copy-start | bytes 388

commit v3 on v2

--- a/solution.py
+++ b/solution.py
@@ -19,7 +19,10 @@
 TILES = X * C // LANES
 TILE = TILES // N_COLS
 MSG = YB * TILE
-GROUPS = (1, 2, 3, 4)
+GROUPS = (2, 4)
+N_Z = 8
+HUB = 15
+LATE = 4
 MESH = pl.DeviceIdType.MESH
 BF = jnp.bfloat16
 F32 = jnp.float32
@@ -142,9 +145,9 @@
 
 
 def kernel(
-    field_ref, dk_ref, pw_ref, pb_ref, vw_ref, vb_ref, ex_ref, own_ref, cell_ref, out_ref,
-    stage, band, dk_pad, hw, vw_pad, vw, send, recv, mid, xs, xr, codes, rows_b, source,
-    near_send, near_recv, far_send, far_recv, mix_send, mix_recv, ex_send, ex_recv,
+    field_hbm, dk_hbm, pw_hbm, pb_hbm, vw_hbm, vb_hbm, ex_hbm, own_hbm, cell_hbm, out_ref,
+    field_ref, dk_ref, pw_ref, pb_ref, vw_ref, vb_ref, ex_ref, own_ref, cell_ref, stage, band, dk_pad, hw, vw_pad, vw, send, recv, mid, xs, xr, codes, rows_b, source,
+    near_send, near_recv, far_send, far_recv, mix_send, mix_recv, ex_send, ex_recv, go, load,
 ):
     r = lax.axis_index("rows")
     me = lax.axis_index("cols")
@@ -153,16 +156,27 @@
     far = lax.rem(r + N_ROWS - 1 + 2 * odd, N_ROWS)
     has_far = jnp.logical_and(r > 0, r < N_ROWS - 1)
     barrier = pltpu.get_barrier_semaphore()
+    loads = [
+        pltpu.make_async_copy(source_ref, target_ref, load.at[i])
+        for i, (source_ref, target_ref) in enumerate(
+            (
+                (field_hbm, field_ref), (ex_hbm, ex_ref), (own_hbm, own_ref), (cell_hbm, cell_ref),
+                (dk_hbm, dk_ref), (pw_hbm, pw_ref), (pb_hbm, pb_ref), (vw_hbm, vw_ref),
+                (vb_hbm, vb_ref),
+            )
+        )
+    ]
+    for copy in loads:
+        copy.start()
 
     for row in (near, far):
         pl.semaphore_signal(barrier, inc=1, device_id={"rows": row}, device_id_type=MESH)
 
-    @pl.loop(1, N_COLS)
-    def _(s):
-        pl.semaphore_signal(
-            barrier, inc=1, device_id={"cols": lax.rem(me + s, N_COLS)}, device_id_type=MESH
-        )
-
+    @pl.when(me != HUB)
+    def _():
+        pl.semaphore_signal(barrier, inc=1, device_id={"cols": HUB}, device_id_type=MESH)
+
+    loads[0].wait()
     stage[...] = field_ref[...].astype(F32)
     for y in range(YB):
         band[3 + y] = stage[pl.ds(y, TILES, stride=YB), :].astype(BF)
@@ -175,7 +189,19 @@
     def _():
         band[7:10] = jnp.zeros((3, TILES, LANES), BF)
 
-    pl.semaphore_wait(barrier, N_COLS + 1)
+    @pl.when(me == HUB)
+    def _():
+        pl.semaphore_wait(barrier, N_COLS + 1)
+
+        @pl.loop(1, N_COLS)
+        def _(s):
+            pl.semaphore_signal(
+                go, inc=1, device_id={"cols": lax.rem(me + s, N_COLS)}, device_id_type=MESH
+            )
+
+    @pl.when(me != HUB)
+    def _():
+        pl.semaphore_wait(barrier, 2)
 
     near_copy = pltpu.make_async_remote_copy(
         src_ref=band.at[pl.ds(4 - odd, 3)], dst_ref=band.at[pl.ds(7 * odd, 3)],
@@ -208,15 +234,23 @@
             far_copy(j).start()
 
     near_copy.start()
+    for copy in loads[1:]:
+        copy.wait()
     pack_exhaust(me, odd, ex_ref, own_ref, cell_ref, xs)
 
-    @pl.loop(1, N_COLS)
-    def _(s):
-        there = lax.rem(me + s, N_COLS)
-        pltpu.make_async_remote_copy(
-            src_ref=xs.at[there], dst_ref=xr.at[me], send_sem=ex_send, recv_sem=ex_recv,
-            device_id={"cols": there}, device_id_type=MESH,
-        ).start()
+    def await_go():
+        @pl.when(me != HUB)
+        def _():
+            pl.semaphore_wait(go, 1)
+
+    def send_exhaust():
+        @pl.loop(1, N_COLS)
+        def _(s):
+            there = lax.rem(me + s, N_COLS)
+            pltpu.make_async_remote_copy(
+                src_ref=xs.at[there], dst_ref=xr.at[me], send_sem=ex_send, recv_sem=ex_recv,
+                device_id={"cols": there}, device_id_type=MESH,
+            ).start()
 
     all_exhaust = pltpu.make_async_remote_copy(
         src_ref=xs.at[0 : N_COLS - 1], dst_ref=xr.at[0 : N_COLS - 1], send_sem=ex_send,
@@ -253,6 +287,13 @@
         mixed = band[3 + y].astype(F32) + jax.nn.gelu(total + bias_h)
         send[:, slot * TILE : (slot + 1) * TILE, :] = mixed.astype(BF).reshape(N_COLS, TILE, LANES)
 
+    late = lax.rem(me, N_Z) >= LATE
+
+    @pl.when(late)
+    def _():
+        await_go()
+        send_exhaust()
+
     near_arrival.wait_recv()
     first = 0
     for slot in range(YB):
@@ -263,6 +304,13 @@
                 far_arrival(slot).wait_recv()
 
         horizontal(slot)
+        if slot + 1 == GROUPS[0]:
+
+            @pl.when(jnp.logical_not(late))
+            def _():
+                await_go()
+                send_exhaust()
+
         if slot + 1 in GROUPS:
             part = slice(first * TILE, (slot + 1) * TILE)
             first = slot + 1
@@ -323,9 +371,18 @@
     out = pl.pallas_call(
         kernel,
         out_shape=jax.ShapeDtypeStruct((Z * MSG, LANES), BF),
-        in_specs=[pl.BlockSpec(memory_space=pltpu.VMEM)] * 9,
+        in_specs=[pl.BlockSpec(memory_space=pltpu.HBM)] * 9,
         out_specs=pl.BlockSpec(memory_space=pltpu.VMEM),
         scratch_shapes=[
+            pltpu.VMEM((TILES * YB, LANES), BF),
+            pltpu.VMEM((KH, KH, C), F32),
+            pltpu.VMEM((C, C), BF),
+            pltpu.VMEM((1, C), F32),
+            pltpu.VMEM((LAYERS, C, KV * C), BF),
+            pltpu.VMEM((LAYERS, C), F32),
+            pltpu.VMEM((C, E_DEV), BF),
+            pltpu.VMEM((1, E_DEV), jnp.int32),
+            pltpu.VMEM((1, E_DEV), jnp.int32),
             pltpu.VMEM((TILES * YB, LANES), F32),
             pltpu.VMEM((YB + 6, TILES, LANES), BF),
             pltpu.VMEM((LANES, LANES), F32),
@@ -348,13 +405,20 @@
             pltpu.SemaphoreType.DMA,
             pltpu.SemaphoreType.DMA,
             pltpu.SemaphoreType.DMA,
+            pltpu.SemaphoreType.REGULAR,
+            pltpu.SemaphoreType.DMA((9,)),
         ],
         compiler_params=pltpu.CompilerParams(
             collective_id=0, has_side_effects=True, vmem_limit_bytes=48 * 1024 * 1024
         ),
     )(
+        *(
+            pltpu.with_memory_space_constraint(a, pltpu.HBM)
+            for a in (
         rows, depth_kernel, point_weight, point_bias.reshape(1, C),
         vert_weight.transpose(0, 2, 1), vert_bias, exhaust.T, owner.reshape(1, E_DEV), cells.reshape(1, E_DEV),
+            )
+        )
     )
     return out.reshape(Z, MSG // YB, YB, LANES).transpose(0, 2, 1, 3).reshape(Z, YB, X * C // N_COLS)
 

time: 43.8 us -> 36.6 us (0.84)
  the two profiles are of different devices: /device:TPU:1 before, /device:TPU:4 now
where the time goes in v3:
time: 36.6 us; the launch traced here: 36.5 us
  Pallas kernels  35.8 us (98%)
  local copies, waits for them, and re-layouts  0.71 us (2%)
    pallas_call x1, Pallas kernels, body(): pl.pallas_call(kernel, out_shape=jax.ShapeDtypeStruct((Z * MSG, LANES), B...  35.8 us

profile of v3, /device:TPU:4, one launch (start us, length us, event | category | flops | bytes accessed | tf_op | source)
XLA Modules:
  0.0 36.5 jit_solution(2563980937356890891)
XLA Ops:
  0.0 35.8 %shard_map.91 = bf16[1024,128]{1,0:T(8,128)(2,1)S(1)} custom-call(bf16[1024,128]{1,0:T(8,128)(2,1)} %bitcast.16, f32[7,7,32]{2,1,0:T(8,128)} %dk_hbm.1, bf16[32,32]{1,0:T(8,128)(2,1)} %pw_hbm.1, f32[1,32]{1,0:T(1,128)} %bitcast.21, bf16[2,32,288]{2,1,0:T(8,128)(2,1)} %bitcast.17, f32[2,32]{1,0:T(2,128)} %vb_hbm.1, bf16[32,512]{1,0:T(8,128)(2,1)} %bitcast.18, ...), custom_call_target="tpu_custom_call" | custom-call | tf_op jit(solution)/shard_map/pallas_call | solution.py:371
  35.8 0.7 %copy.13 = bf16[32,4,1024]{2,1,0:T(4,128)(2,1)} copy(bf16[32,4,1024]{2,1,0:T(4,128)(2,1)S(1)} %bitcast.15) | data formatting | bytes 524288

commit v4 on v3

--- a/solution.py
+++ b/solution.py
@@ -22,6 +22,7 @@
 GROUPS = (2, 4)
 N_Z = 8
 HUB = 15
+PAIRS = 16
 LATE = 4
 MESH = pl.DeviceIdType.MESH
 BF = jnp.bfloat16
@@ -139,9 +140,12 @@
         for k in range(KV):
             part = wide[k * C : (k + 1) * C, :]
             whole = jnp.concatenate([part, part, part, part], axis=0)
-            vw[layer, k * LANES : (k + 1) * LANES, :] = jnp.where(
-                row // C == lane // C, whole, 0.0
-            ).astype(BF)
+            block = jnp.where(row // C == lane // C, whole, 0.0).astype(BF)
+            vw[layer, k * LANES : (k + 1) * LANES, 0:LANES] = block
+            vw[layer, (k + 1) * LANES : (k + 2) * LANES, LANES : 2 * LANES] = block
+        empty = jnp.zeros((LANES, LANES), BF)
+        vw[layer, KV * LANES : (KV + 1) * LANES, 0:LANES] = empty
+        vw[layer, 0:LANES, LANES : 2 * LANES] = empty
 
 
 def kernel(
@@ -330,28 +334,40 @@
     all_mixed.wait_recv()
 
     def conv(buffer, layer, block):
+        levels = buffer[pl.ds(block * 2 * PAIRS, 2 * PAIRS + 8)].reshape(PAIRS + 4, 2, MSG, LANES)
         rows = jnp.concatenate(
-            [buffer[pl.ds(block * 8 + k, 8)].reshape(8 * MSG, LANES) for k in range(KV)], axis=1
-        )
-        before = buffer[pl.ds(block * 8 + 4, 8)].reshape(8 * MSG, LANES).astype(F32)
-        return before + jax.nn.gelu(dot(rows, vw[layer]) + bias_v[layer : layer + 1])
-
-    @pl.loop(0, 4)
+            [levels[k // 2 : k // 2 + PAIRS, k % 2].reshape(PAIRS * MSG, LANES) for k in range(KV + 1)],
+            axis=1,
+        )
+        wide = dot(rows, vw[layer])
+        result = [
+            levels[2 : 2 + PAIRS, j].astype(F32)
+            + jax.nn.gelu(
+                wide[:, j * LANES : (j + 1) * LANES] + bias_v[layer : layer + 1]
+            ).reshape(PAIRS, MSG, LANES)
+            for j in range(2)
+        ]
+        return jnp.stack(result, axis=1).reshape(2 * PAIRS, MSG, LANES)
+
+    blocks = Z // (2 * PAIRS)
+    size = 2 * PAIRS * MSG
+
+    @pl.loop(0, blocks)
     def _(block):
-        mid[pl.ds(block * 8 + 4, 8)] = conv(recv, 0, block).astype(BF).reshape(8, MSG, LANES)
-
-    @pl.loop(0, 4)
+        mid[pl.ds(block * 2 * PAIRS + 4, 2 * PAIRS)] = conv(recv, 0, block).astype(BF)
+
+    @pl.loop(0, blocks)
     def _(block):
-        base = pl.multiple_of(block * 256, 256)
-        result = conv(mid, 1, block) + source[pl.ds(base, 256), :]
-        for level in range(8):
+        base = pl.multiple_of(block * size, size)
+        result = conv(mid, 1, block).reshape(size, LANES) + source[pl.ds(base, size), :]
+        for level in range(2 * PAIRS):
             for slot in range(YB):
                 y = odd * slot + (1 - odd) * (3 - slot)
                 start = level * MSG + slot * TILE
                 stage[pl.ds(base + level * MSG + y, TILE, stride=YB), :] = result[
                     start : start + TILE
                 ]
-        out_ref[pl.ds(base, 256), :] = stage[pl.ds(base, 256), :].astype(BF)
+        out_ref[pl.ds(base, size), :] = stage[pl.ds(base, size), :].astype(BF)
 
     near_copy.wait_send()
 
@@ -388,7 +404,7 @@
             pltpu.VMEM((LANES, LANES), F32),
             pltpu.VMEM((KH * LANES, 3 * LANES), BF),
             pltpu.VMEM((LANES, 3 * LANES), F32),
-            pltpu.VMEM((LAYERS, KV * LANES, LANES), BF),
+            pltpu.VMEM((LAYERS, (KV + 1) * LANES, 2 * LANES), BF),
             pltpu.VMEM((N_COLS, MSG, LANES), BF),
             pltpu.VMEM((Z + 8, MSG, LANES), BF),
             pltpu.VMEM((Z + 8, MSG, LANES), BF),

time: 36.6 us -> 35.5 us (0.970)
  Pallas kernels: 35.8 us -> 34.7 us
    pallas_call x1, Pallas kernels: 35.8 us -> 34.7 us  [body(): pl.pallas_call(kernel, out_shape=jax.ShapeDtypeStruct((Z * MSG, LANES), B...]
where the time goes in v4:
time: 35.5 us; the launch traced here: 35.4 us
  Pallas kernels  34.7 us (98%)
  local copies, waits for them, and re-layouts  0.71 us (2%)
    pallas_call x1, Pallas kernels, body(): pl.pallas_call(kernel, out_shape=jax.ShapeDtypeStruct((Z * MSG, LANES), B...  34.7 us

profile of v4, /device:TPU:4, one launch (start us, length us, event | category | flops | bytes accessed | tf_op | source)
XLA Modules:
  0.0 35.4 jit_solution(6194067650845867800)
XLA Ops:
  0.0 34.7 %shard_map.91 = bf16[1024,128]{1,0:T(8,128)(2,1)S(1)} custom-call(bf16[1024,128]{1,0:T(8,128)(2,1)} %bitcast.16, f32[7,7,32]{2,1,0:T(8,128)} %dk_hbm.1, bf16[32,32]{1,0:T(8,128)(2,1)} %pw_hbm.1, f32[1,32]{1,0:T(1,128)} %bitcast.21, bf16[2,32,288]{2,1,0:T(8,128)(2,1)} %bitcast.17, f32[2,32]{1,0:T(2,128)} %vb_hbm.1, bf16[32,512]{1,0:T(8,128)(2,1)} %bitcast.18, ...), custom_call_target="tpu_custom_call" | custom-call | tf_op jit(solution)/shard_map/pallas_call | solution.py:387
  34.7 0.7 %copy.13 = bf16[32,4,1024]{2,1,0:T(4,128)(2,1)} copy(bf16[32,4,1024]{2,1,0:T(4,128)(2,1)S(1)} %bitcast.15) | data formatting | bytes 524288
